TPU v7x, 32 devices: a whole 2x2x4 slice. The times are simulated.
32 devices in a mesh: dp: 8 (over z, y), mp: 4 (over x, core).
Axes of the slice: x: 2, y: 2, z: 4, core: 2. Of those that a mesh axis runs over, the one named last changes fastest.
Arguments:
- tokens: bfloat16 [8192, 768], P(('dp', 'mp')), may hold values from -6 to 6
- segment_ids: int32 [8192], P('dp'), may hold values from 0 to 10, as said below
- keep_mask: int32 [88, 2], P('dp'), may hold values 0 or 1
- first_gain: bfloat16 [768], replicated, may hold values from 0.5 to 1.5
- first_shift: bfloat16 [768], replicated, may hold values from -3 to 3
- query_weight: bfloat16 [768, 768], P(None, 'mp'), may hold values from -0.21875 to 0.21875
- query_bias: bfloat16 [768], P('mp'), may hold values from -3 to 3
- key_weight: bfloat16 [768, 768], P(None, 'mp'), may hold values from -0.21875 to 0.21875
- value_weight: bfloat16 [768, 768], P(None, 'mp'), may hold values from -0.21875 to 0.21875
- value_bias: bfloat16 [768], P('mp'), may hold values from -3 to 3
- out_weight: bfloat16 [768, 768], P('mp'), may hold values from -2.5 to 2.5
- out_bias: bfloat16 [768], replicated, may hold values from -2 to 2
- second_gain: bfloat16 [768], replicated, may hold values from 0.5 to 1.5
- second_shift: bfloat16 [768], replicated, may hold values from -3 to 3
- up_weight: bfloat16 [768, 3072], P(None, 'mp'), may hold values from -0.21875 to 0.21875
- up_bias: bfloat16 [3072], P('mp'), may hold values from -3 to 3
- down_weight: bfloat16 [3072, 768], P('mp'), may hold values from -0.109375 to 0.109375
- down_bias: bfloat16 [768], replicated, may hold values from -2 to 2
- cotangent: bfloat16 [8192, 768], P(('dp', 'mp')), may hold values from -6 to 6
Outputs:
- layer_out: bfloat16 [8192, 768], P(('dp', 'mp'))
- input_grad: float32 [8192, 768], P(('dp', 'mp'))
- first_gain_grad: float32 [768], replicated
- first_shift_grad: float32 [768], replicated
- query_weight_grad: float32 [768, 768], P(None, 'mp')
- query_bias_grad: float32 [768], P('mp')
- key_weight_grad: float32 [768, 768], P(None, 'mp')
- value_weight_grad: float32 [768, 768], P(None, 'mp')
- value_bias_grad: float32 [768], P('mp')
- out_weight_grad: float32 [768, 768], P('mp')
- out_bias_grad: float32 [768], replicated
- second_gain_grad: float32 [768], replicated
- second_shift_grad: float32 [768], replicated
- up_weight_grad: float32 [768, 3072], P(None, 'mp')
- up_bias_grad: float32 [3072], P('mp')
- down_weight_grad: float32 [3072, 768], P('mp')
- down_bias_grad: float32 [768], replicated
Inputs may be any that keep to these rules, and one draw needn't show every extreme that they name: `segment_ids`: within each aligned block of 1024 tokens the ids start at 0, never fall and rise by one from image to image; every image but the last of a block has 102, 198 or 578 tokens, the last holds the remaining tokens. In the first block every image but the last has 102 tokens. `keep_mask`: row i of a block of 11 rows belongs to the image with segment id i of the same index of dp.
All inputs are finite; a program needn't handle non-finite values.
Results may differ from a plain program's by a relative error of at most 0.02.
Values may be sent and summed in bfloat16 or wider, within the bound.
No kernel may reach another device: no remote copies, remote signals or barrier semaphores. Data moves between devices by JAX's collectives and lax.ppermute only.
A program may use at most 128 MiB of HBM per device.

v0:
```python
import math
import jax
import jax.numpy as jnp
from jax import lax
from jax.sharding import PartitionSpec as P

HD = 64
eps = 1e-06


def layer_norm(values, scaling, bias_add):
    center = values - jnp.mean(values, axis=-1, keepdims=True)
    spread = jnp.mean(center * center, axis=-1, keepdims=True)
    return center * lax.rsqrt(spread + eps) * scaling + bias_add


def gelu_exact(values):
    return jax.nn.gelu(values, approximate=False)


def per_device(
    tokens,
    segment_ids,
    keep_mask,
    first_gain,
    first_shift,
    query_weight,
    query_bias,
    key_weight,
    value_weight,
    value_bias,
    out_weight,
    out_bias,
    second_gain,
    second_shift,
    up_weight,
    up_bias,
    down_weight,
    down_bias,
    cotangent,
):
    f32 = jnp.float32
    bf16 = jnp.bfloat16
    local_rows = tokens.shape[0]
    row_count = segment_ids.shape[0]
    head_width = query_weight.shape[1]
    head_group = head_width // HD
    score_scale = 1.0 / math.sqrt(HD)
    block_rows = min(512, row_count)
    block_count = row_count // block_rows
    offset = lax.axis_index("mp") * local_rows
    local_ids = lax.dynamic_slice_in_dim(segment_ids, offset, local_rows)
    onehot = (
        local_ids[:, None] == jnp.arange(keep_mask.shape[0], dtype=jnp.int32)[None, :]
    ).astype(f32)
    keep_rows = jnp.dot(onehot, keep_mask.astype(f32), precision=lax.Precision.HIGHEST) / 0.9
    allowed = segment_ids[:, None] == segment_ids[None, :]
    gain_one = first_gain.astype(f32)
    shift_one = first_shift.astype(f32)
    gain_two = second_gain.astype(f32)
    shift_two = second_shift.astype(f32)
    inputs = tokens.astype(f32)
    normed = layer_norm(inputs, gain_one, shift_one).astype(bf16)
    normed_all = lax.all_gather(normed, "mp", axis=0, tiled=True)
    query_rows = (
        jnp.dot(normed_all, query_weight, preferred_element_type=f32) + query_bias.astype(f32)
    ).astype(bf16)
    key_rows = jnp.dot(normed_all, key_weight, preferred_element_type=f32).astype(bf16)
    value_rows = (
        jnp.dot(normed_all, value_weight, preferred_element_type=f32) + value_bias.astype(f32)
    ).astype(bf16)
    key_heads = key_rows.reshape(row_count, head_group, HD)
    value_heads = value_rows.reshape(row_count, head_group, HD)
    context_parts = []
    lse_parts = []
    for number in range(block_count):
        row_start = number * block_rows
        query_block = query_rows[row_start : row_start + block_rows].reshape(
            block_rows, head_group, HD
        )
        scores = (
            jnp.einsum("qhd,khd->hqk", query_block, key_heads, preferred_element_type=f32)
            * score_scale
        )
        scores = jnp.where(allowed[row_start : row_start + block_rows][None], scores, -1e30)
        largest = jnp.max(scores, axis=-1, keepdims=True)
        powers = jnp.exp(scores - largest)
        totals = jnp.sum(powers, axis=-1, keepdims=True)
        weights = (powers / totals).astype(bf16)
        context_block = jnp.einsum("hqk,khd->qhd", weights, value_heads, preferred_element_type=f32)
        context_parts.append(context_block.reshape(block_rows, head_width))
        lse_parts.append(largest + jnp.log(totals))
    context = jnp.concatenate(context_parts, axis=0).astype(bf16)
    attended = lax.psum_scatter(
        jnp.dot(context, out_weight, preferred_element_type=f32).astype(jnp.bfloat16),
        "mp",
        scatter_dimension=0,
        tiled=True,
    ).astype(jnp.float32) + out_bias.astype(f32)
    middle = inputs + keep_rows[:, 0:1] * attended
    normed_two = layer_norm(middle, gain_two, shift_two).astype(bf16)
    normed_two_all = lax.all_gather(normed_two, "mp", axis=0, tiled=True)
    hidden = jnp.dot(normed_two_all, up_weight, preferred_element_type=f32) + up_bias.astype(f32)
    activated = gelu_exact(hidden).astype(bf16)
    mlp_out = lax.psum_scatter(
        jnp.dot(activated, down_weight, preferred_element_type=f32).astype(jnp.bfloat16),
        "mp",
        scatter_dimension=0,
        tiled=True,
    ).astype(jnp.float32) + down_bias.astype(f32)
    layer_out = (middle + keep_rows[:, 1:2] * mlp_out).astype(bf16)
    out_grad = cotangent.astype(f32)
    mlp_grad = out_grad * keep_rows[:, 1:2]
    down_bias_grad = jnp.sum(mlp_grad, axis=0)
    mlp_grad_all = lax.all_gather(mlp_grad.astype(bf16), "mp", axis=0, tiled=True)
    down_weight_grad = jnp.einsum("rf,rd->fd", activated, mlp_grad_all, preferred_element_type=f32)
    act_grad = jnp.einsum("rd,fd->rf", mlp_grad_all, down_weight, preferred_element_type=f32)
    unused_value, gelu_pull = jax.vjp(gelu_exact, hidden)
    hidden_grad = gelu_pull(act_grad)[0].astype(bf16)
    up_bias_grad = jnp.sum(hidden_grad.astype(f32), axis=0)
    up_weight_grad = jnp.einsum(
        "rd,rf->df", normed_two_all, hidden_grad, preferred_element_type=f32
    )
    second_grad = lax.psum_scatter(
        jnp.einsum("rf,df->rd", hidden_grad, up_weight, preferred_element_type=f32).astype(
            jnp.bfloat16
        ),
        "mp",
        scatter_dimension=0,
        tiled=True,
    ).astype(jnp.float32)
    unused_value, norm_pull_two = jax.vjp(layer_norm, middle, gain_two, shift_two)
    middle_part, gain_two_grad, shift_two_grad = norm_pull_two(second_grad)
    middle_grad = out_grad + middle_part
    attn_grad = middle_grad * keep_rows[:, 0:1]
    out_bias_grad = jnp.sum(attn_grad, axis=0)
    attn_grad_all = lax.all_gather(attn_grad.astype(bf16), "mp", axis=0, tiled=True)
    out_weight_grad = jnp.einsum("rc,rd->cd", context, attn_grad_all, preferred_element_type=f32)
    context_grad = jnp.einsum(
        "rd,cd->rc", attn_grad_all, out_weight, preferred_element_type=f32
    ).astype(bf16)
    context_grad_heads = context_grad.reshape(row_count, head_group, HD)
    query_grads = []
    key_grad = jnp.zeros((row_count, head_group, HD), f32)
    value_grad = jnp.zeros((row_count, head_group, HD), f32)
    for number in range(block_count):
        row_start = number * block_rows
        query_block = query_rows[row_start : row_start + block_rows].reshape(
            block_rows, head_group, HD
        )
        scores = (
            jnp.einsum("qhd,khd->hqk", query_block, key_heads, preferred_element_type=f32)
            * score_scale
        )
        scores = jnp.where(allowed[row_start : row_start + block_rows][None], scores, -1e30)
        probs = jnp.exp(scores - lse_parts[number])
        grad_block = context_grad_heads[row_start : row_start + block_rows]
        prob_grad = jnp.einsum("qhd,khd->hqk", grad_block, value_heads, preferred_element_type=f32)
        center = jnp.sum(probs * prob_grad, axis=-1, keepdims=True)
        score_grad = (probs * (prob_grad - center)).astype(bf16)
        query_grads.append(
            jnp.einsum("hqk,khd->qhd", score_grad, key_heads, preferred_element_type=f32)
            * score_scale
        )
        key_grad = (
            key_grad
            + jnp.einsum("hqk,qhd->khd", score_grad, query_block, preferred_element_type=f32)
            * score_scale
        )
        value_grad = value_grad + jnp.einsum(
            "hqk,qhd->khd", probs.astype(bf16), grad_block, preferred_element_type=f32
        )
    query_grad_rows = (
        jnp.concatenate(query_grads, axis=0).reshape(row_count, head_width).astype(bf16)
    )
    key_grad_rows = key_grad.reshape(row_count, head_width).astype(bf16)
    value_grad_rows = value_grad.reshape(row_count, head_width).astype(bf16)
    query_bias_grad = jnp.sum(query_grad_rows.astype(f32), axis=0)
    value_bias_grad = jnp.sum(value_grad_rows.astype(f32), axis=0)
    query_weight_grad = jnp.einsum(
        "rd,rc->dc", normed_all, query_grad_rows, preferred_element_type=f32
    )
    key_weight_grad = jnp.einsum("rd,rc->dc", normed_all, key_grad_rows, preferred_element_type=f32)
    value_weight_grad = jnp.einsum(
        "rd,rc->dc", normed_all, value_grad_rows, preferred_element_type=f32
    )
    total = jnp.einsum("rc,dc->rd", query_grad_rows, query_weight, preferred_element_type=f32)
    total = total + jnp.einsum("rc,dc->rd", key_grad_rows, key_weight, preferred_element_type=f32)
    first_grad = lax.psum_scatter(
        (
            total
            + jnp.einsum("rc,dc->rd", value_grad_rows, value_weight, preferred_element_type=f32)
        ).astype(jnp.bfloat16),
        "mp",
        scatter_dimension=0,
        tiled=True,
    ).astype(jnp.float32)
    unused_value, norm_pull_one = jax.vjp(layer_norm, inputs, gain_one, shift_one)
    input_part, gain_one_grad, shift_one_grad = norm_pull_one(first_grad)
    input_grad = middle_grad + input_part
    (
        query_weight_grad,
        query_bias_grad,
        key_weight_grad,
        value_weight_grad,
        value_bias_grad,
        out_weight_grad,
        up_weight_grad,
        up_bias_grad,
        down_weight_grad,
    ) = lax.psum(
        (
            query_weight_grad,
            query_bias_grad,
            key_weight_grad,
            value_weight_grad,
            value_bias_grad,
            out_weight_grad,
            up_weight_grad,
            up_bias_grad,
            down_weight_grad,
        ),
        "dp",
    )
    gain_one_grad, shift_one_grad, out_bias_grad, gain_two_grad, shift_two_grad, down_bias_grad = (
        lax.psum(
            (
                gain_one_grad,
                shift_one_grad,
                out_bias_grad,
                gain_two_grad,
                shift_two_grad,
                down_bias_grad,
            ),
            ("dp", "mp"),
        )
    )
    return (
        layer_out,
        input_grad,
        gain_one_grad,
        shift_one_grad,
        query_weight_grad,
        query_bias_grad,
        key_weight_grad,
        value_weight_grad,
        value_bias_grad,
        out_weight_grad,
        out_bias_grad,
        gain_two_grad,
        shift_two_grad,
        up_weight_grad,
        up_bias_grad,
        down_weight_grad,
        down_bias_grad,
    )


def solution(mesh):
    in_specs = (
        P(("dp", "mp"), None),
        P("dp"),
        P("dp", None),
        P(),
        P(),
        P(None, "mp"),
        P("mp"),
        P(None, "mp"),
        P(None, "mp"),
        P("mp"),
        P("mp", None),
        P(),
        P(),
        P(),
        P(None, "mp"),
        P("mp"),
        P("mp", None),
        P(),
        P(("dp", "mp"), None),
    )
    out_specs = (
        P(("dp", "mp"), None),
        P(("dp", "mp"), None),
        P(),
        P(),
        P(None, "mp"),
        P("mp"),
        P(None, "mp"),
        P(None, "mp"),
        P("mp"),
        P("mp", None),
        P(),
        P(),
        P(),
        P(None, "mp"),
        P("mp"),
        P("mp", None),
        P(),
    )
    return jax.shard_map(
        per_device, mesh=mesh, in_specs=in_specs, out_specs=out_specs, check_vma=False
    )
```

profile of v0, /device:TPU:0, one launch (start us, length us, event | category | flops | bytes accessed | tf_op | source)
XLA Modules:
  0.0 535.1 jit_solution(10001136210454369403)
XLA Ops:
  11.7 2.0 fusion.43
  17.6 18.7 %all-gather.5.cloned.1.call-done = bf16[1024,768]{1,0:T(8,128)(2,1)} async-done(((bf16[256,768]{1,0:T(8,128)(2,1)}), bf16[1024,768]{1,0:T(8,128)(2,1)}) %all-gather.5.cloned.1.call-update) | async-done | bytes 1572880 | tf_op jit(solution)/shard_map/all_gather | solution.py:64
  36.2 2.3 fusion.27
  58.1 23.9 %reduce-scatter.5.cloned.1.call-done = bf16[256,768]{1,0:T(8,128)(2,1)} async-done(((bf16[1024,768]{1,0:T(8,128)(2,1)}), bf16[256,768]{1,0:T(8,128)(2,1)}) %reduce-scatter.5.cloned.1.call-update) | async-done | bytes 393232 | tf_op jit(solution)/shard_map/reduce_scatter | solution.py:94
  85.9 2.0 add_convert_fusion.3
  90.8 16.9 %all-gather.7.cloned.1.call-done = bf16[1024,768]{1,0:T(8,128)(2,1)} async-done(((bf16[256,768]{1,0:T(8,128)(2,1)}), bf16[1024,768]{1,0:T(8,128)(2,1)}) %all-gather.7.cloned.1.call-update) | async-done | bytes 1572880 | tf_op jit(solution)/shard_map/all_gather | solution.py:102
  107.7 4.8 fusion.66
  112.5 16.9 %all-gather.9.cloned.1.call-done = bf16[1024,768]{1,0:T(8,128)(2,1)} async-done(((bf16[256,768]{1,0:T(8,128)(2,1)}), bf16[1024,768]{1,0:T(8,128)(2,1)}) %all-gather.9.cloned.1.call-update) | async-done | bytes 1572880 | tf_op jit(solution)/shard_map/all_gather | solution.py:115
  129.4 11.8 %convert_reduce_fusion = (f32[768]{0:T(1024)}, bf16[1024,768]{1,0:T(8,128)(2,1)S(1)}, f32[1024,768]{1,0:T(8,128)}) fusion(f32[1024,768]{1,0:T(8,128)} %fusion.66, f32[768]{0:T(1024)S(1)} %convert_element_type.170, bf16[1024,768]{1,0:T(8,128)(2,1)} %all-gather.9.cloned.1.call-done, bf16[768,768]{1,0:T(8,128)(2,1)S(1)} %copy-done), kind=kOutput, calls=%fused_computation.20 | convolution fusion | flops 1266941184 | bytes 10622976 | tf_op jit(solution)/shard_map/rd,fd->rf/dot_general | solution.py:117
  142.4 2.6 convolution_convert_fusion
  145.0 3.3 multiply_convert_fusion.2
  149.5 2.5 convolution_convert_fusion.1
  153.5 19.7 %reduce-scatter.9.cloned.1.call-done = bf16[256,768]{1,0:T(8,128)(2,1)} async-done(((bf16[1024,768]{1,0:T(8,128)(2,1)}), bf16[256,768]{1,0:T(8,128)(2,1)}) %reduce-scatter.9.cloned.1.call-update) | async-done | bytes 393232 | tf_op jit(solution)/shard_map/reduce_scatter | solution.py:124
  173.1 2.1 fusion.47
  176.5 27.7 %reduce-scatter.7.cloned.1.call-done = bf16[256,768]{1,0:T(8,128)(2,1)} async-done(((bf16[1024,768]{1,0:T(8,128)(2,1)}), bf16[256,768]{1,0:T(8,128)(2,1)}) %reduce-scatter.7.cloned.1.call-update) | async-done | bytes 393232 | tf_op jit(solution)/shard_map/reduce_scatter | solution.py:105
  204.2 2.6 fusion.59
  206.8 2.4 fusion.36
  210.8 18.1 %all-gather.11.cloned.1.call-done = bf16[1024,768]{1,0:T(8,128)(2,1)} async-done(((bf16[256,768]{1,0:T(8,128)(2,1)}), bf16[1024,768]{1,0:T(8,128)(2,1)}) %all-gather.11.cloned.1.call-update) | async-done | bytes 1572880 | tf_op jit(solution)/shard_map/all_gather | solution.py:137
  229.0 2.1 convolution_convert_fusion.3
  231.1 3.9 multiply_reduce_fusion.1
  240.2 1.9 multiply_reduce_fusion
  242.1 1.8 convert_reduce_fusion.4
  249.6 1.8 add_convert_fusion
  251.7 4.9 fusion.71
  256.6 2.8 fusion.70
  265.5 22.2 %all-reduce.1 = (f32[192]{0:T(256)}, f32[192]{0:T(256)}, f32[768]{0:T(1024)}) all-reduce(f32[192]{0:T(256)S(1)} %reduce_sum.217, f32[192]{0:T(256)S(1)} %reduce_sum.219, f32[768]{0:T(1024)S(1)} %copy-done.58), channel_id=1, replica_groups=mesh['dp'=8,'mp'=4] {'dp'}, use_global_device_ids=true, to_apply=%region_24.25 | all-reduce | flops 1152 | bytes 9216 | tf_op jit(solution)/shard_map/psum | solution.py:211
  290.6 41.8 %all-reduce = (f32[768]{0:T(1024)}, f32[768]{0:T(1024)}, f32[768]{0:T(1024)}, f32[768]{0:T(1024)}, f32[768]{0:T(1024)}, /*index=5*/f32[768]{0:T(1024)}) all-reduce(f32[768]{0:T(1024)S(1)} %get-tuple-element.19, f32[768]{0:T(1024)S(1)} %get-tuple-element.24, f32[768]{0:T(1024)S(1)} %copy-done.50, ...), channel_id=1, replica_groups=mesh['dp'=8,'mp'=4] {'dp','mp'}, use_global_device_ids=true, to_apply=%region_19.20 | all-reduce | flops 4608 | bytes 36864 | tf_op jit(solution)/shard_map/psum | solution.py:226
  332.3 2.3 add_add_fusion.2
  334.6 184.2 %all-reduce.5.cloned.1.call-done = (f32[768,192]{0,1:T(8,128)}, f32[768,192]{0,1:T(8,128)}, f32[768,192]{0,1:T(8,128)}, f32[192,768]{1,0:T(8,128)}, f32[768,768]{1,0:T(8,128)}, /*index=5*/f32[768,768]{1,0:T(8,128)}) async-done(((f32[768,192]{0,1:T(8,128)}, f32[768,192]{0,1:T(8,128)}, f32[768,192]{0,1:T(8,128)}, f32[192,768]{1,0:T(8,128)}, f32[768,768]{1,0:T(8,128)}, /*index=5*/f32[768,768]{1,0:T(8,128)}), ...) | async-done | bytes 7077904 | tf_op jit(solution)/shard_map/psum | solution.py:211
  518.8 2.1 copy.42
  520.9 1.9 copy.43
  522.8 1.9 copy.44
  (218 shorter events, 64.4 us)
Async XLA Ops:
  7.2 122.2 %copy-start = (bf16[768,768]{1,0:T(8,128)(2,1)S(1)}, bf16[768,768]{1,0:T(8,128)(2,1)}, u32[]{:S(2)}) copy-start(bf16[768,768]{1,0:T(8,128)(2,1)} %param.35) | copy-start | bytes 3538948
  7.2 29.0 %all-gather.5.cloned.1.call-start = ((), (), s32[]{:S(2)}) async-start(), calls=%async_computation.4 | async-start | bytes 1966080 | tf_op jit(solution)/shard_map/all_gather | solution.py:64
  8.5 6.0 %copy-start.40 = (f32[256]{0:T(256)}, f32[256]{0:T(256)S(1)}, u32[]{:S(2)}) copy-start(f32[256]{0:T(256)S(1)} %broadcast_multiply_fusion.1) | copy-start | bytes 3076
  13.7 68.3 %reduce-scatter.5.cloned.1.call-start = ((), (), s32[]{:S(2)}) async-start(), calls=%async_computation.5 | async-start | bytes 1966080 | tf_op jit(solution)/shard_map/reduce_scatter | solution.py:94
  15.1 23.4 %copy-start.34 = (bf16[768,192]{0,1:T(8,128)(2,1)S(1)}, bf16[768,192]{0,1:T(8,128)(2,1)}, u32[]{:S(2)}) copy-start(bf16[768,192]{0,1:T(8,128)(2,1)} %param.26) | copy-start | bytes 884740
  38.6 6.5 %copy-start.16 = (bf16[512,192]{0,1:T(8,128)(2,1)}, bf16[512,192]{0,1:T(8,128)(2,1)S(1)}, u32[]{:S(2)}) copy-start(bf16[512,192]{0,1:T(8,128)(2,1)S(1)} %get-tuple-element.55) | copy-start | bytes 589828
  45.0 6.4 %copy-start.26 = (bf16[3,64,512]{2,1,0:T(8,128)(2,1)}, bf16[3,64,512]{2,1,0:T(8,128)(2,1)S(1)}, u32[]{:S(2)}) copy-start(bf16[3,64,512]{2,1,0:T(8,128)(2,1)S(1)} %fusion.35) | copy-start | bytes 589828
  51.4 30.7 %copy-start.4 = (bf16[256,768]{1,0:T(8,128)(2,1)S(1)}, bf16[256,768]{1,0:T(8,128)(2,1)}, u32[]{:S(2)}) copy-start(bf16[256,768]{1,0:T(8,128)(2,1)} %param.19) | copy-start | bytes 1179652
  52.0 35.9 %copy-start.11 = (bf16[256,768]{1,0:T(8,128)(2,1)S(1)}, bf16[256,768]{1,0:T(8,128)(2,1)}, u32[]{:S(2)}) copy-start(bf16[256,768]{1,0:T(8,128)(2,1)} %param.37) | copy-start | bytes 1179652
  53.8 53.9 %all-gather.7.cloned.1.call-start = ((), (), s32[]{:S(2)}) async-start(), calls=%async_computation.6 | async-start | bytes 1966080 | tf_op jit(solution)/shard_map/all_gather | solution.py:102
  87.9 41.4 %all-gather.9.cloned.1.call-start = ((), (), s32[]{:S(2)}) async-start(), calls=%async_computation.8 | async-start | bytes 1966080 | tf_op jit(solution)/shard_map/all_gather | solution.py:115
  89.6 83.6 %reduce-scatter.9.cloned.1.call-start = ((), (), s32[]{:S(2)}) async-start(), calls=%async_computation.9 | async-start | bytes 1966080 | tf_op jit(solution)/shard_map/reduce_scatter | solution.py:124
  129.4 13.0 %copy-start.61 = (bf16[768,768]{1,0:T(8,128)(2,1)S(1)}, bf16[768,768]{1,0:T(8,128)(2,1)}, u32[]{:S(2)}) copy-start(bf16[768,768]{1,0:T(8,128)(2,1)} %param.33) | copy-start | bytes 3538948
  145.0 59.2 %reduce-scatter.7.cloned.1.call-start = ((), (), s32[]{:S(2)}) async-start(), calls=%async_computation.7 | async-start | bytes 1966080 | tf_op jit(solution)/shard_map/reduce_scatter | solution.py:105
  149.5 23.7 %copy-start.6 = (bf16[256,768]{1,0:T(8,128)(2,1)S(1)}, bf16[256,768]{1,0:T(8,128)(2,1)}, u32[]{:S(2)}) copy-start(bf16[256,768]{1,0:T(8,128)(2,1)} %reduce-scatter.5.cloned.1.call-done) | copy-start | bytes 1179652
  152.0 54.8 %copy-start.12 = (bf16[256,768]{1,0:T(8,128)(2,1)S(1)}, bf16[256,768]{1,0:T(8,128)(2,1)}, u32[]{:S(2)}) copy-start(bf16[256,768]{1,0:T(8,128)(2,1)} %param.37) | copy-start | bytes 1179652
  152.0 76.9 %all-gather.11.cloned.1.call-start = ((), (), s32[]{:S(2)}) async-start(), calls=%async_computation.10 | async-start | bytes 1966080 | tf_op jit(solution)/shard_map/all_gather | solution.py:137
  206.8 24.3 %copy-start.23 = (bf16[1024,192]{0,1:T(8,128)(2,1)S(1)}, bf16[1024,192]{0,1:T(8,128)(2,1)}, u32[]{:S(2)}) copy-start(bf16[1024,192]{0,1:T(8,128)(2,1)} %copy-done.22) | copy-start | bytes 1179652
  209.2 78.5 %reduce-scatter.11.cloned.1.call-start = ((), (), s32[]{:S(2)}) async-start(), calls=%async_computation.11 | async-start | bytes 1966080 | tf_op jit(solution)/shard_map/reduce_scatter | solution.py:189
  251.4 267.4 %all-reduce.5.cloned.1.call-start = ((), (), s32[]{:S(2)}) async-start(), calls=%async_computation.12 | async-start | bytes 14155776 | tf_op jit(solution)/shard_map/psum | solution.py:211
  264.7 23.0 %copy-start.38 = (f32[768]{0:T(1024)S(1)}, f32[768]{0:T(1024)}, u32[]{:S(2)}) copy-start(f32[768]{0:T(1024)} %copy-done.37) | copy-start | bytes 9220
  264.7 23.0 %copy-start.41 = (f32[256]{0:T(256)S(1)}, f32[256]{0:T(256)}, u32[]{:S(2)}) copy-start(f32[256]{0:T(256)} %copy-done.40) | copy-start | bytes 3076
  264.7 24.3 %copy-start.55 = (f32[256]{0:T(256)S(1)}, f32[256]{0:T(256)}, u32[]{:S(2)}) copy-start(f32[256]{0:T(256)} %copy-done.54) | copy-start | bytes 3076
  264.7 24.3 %copy-start.46 = (f32[256]{0:T(256)S(1)}, f32[256]{0:T(256)}, u32[]{:S(2)}) copy-start(f32[256]{0:T(256)} %copy-done.45) | copy-start | bytes 3076
  264.7 25.8 %copy-start.47 = (f32[768]{0:T(1024)S(1)}, f32[768]{0:T(1024)}, u32[]{:S(2)}) copy-start(f32[768]{0:T(1024)} %get-tuple-element.17) | copy-start | bytes 9220
  264.7 25.8 %copy-start.48 = (f32[768]{0:T(1024)S(1)}, f32[768]{0:T(1024)}, u32[]{:S(2)}) copy-start(f32[768]{0:T(1024)} %get-tuple-element.23) | copy-start | bytes 9220
  264.7 25.8 %copy-start.49 = (f32[768]{0:T(1024)S(1)}, f32[768]{0:T(1024)}, u32[]{:S(2)}) copy-start(f32[768]{0:T(1024)} %get-tuple-element.21) | copy-start | bytes 9220
  264.7 25.8 %copy-start.50 = (f32[768]{0:T(1024)S(1)}, f32[768]{0:T(1024)}, u32[]{:S(2)}) copy-start(f32[768]{0:T(1024)} %get-tuple-element.22) | copy-start | bytes 9220
  264.7 67.6 %copy-start.13 = (bf16[256,768]{1,0:T(8,128)(2,1)S(1)}, bf16[256,768]{1,0:T(8,128)(2,1)}, u32[]{:S(2)}) copy-start(bf16[256,768]{1,0:T(8,128)(2,1)} %param.37) | copy-start | bytes 1179652
  264.8 67.6 %copy-start.53 = (f32[256]{0:T(256)S(1)}, f32[256]{0:T(256)}, u32[]{:S(2)}) copy-start(f32[256]{0:T(256)} %copy-done.52) | copy-start | bytes 3076
  518.8 5.9 %copy-start.30 = (f32[192,768]{1,0:T(8,128)S(1)}, f32[192,768]{1,0:T(8,128)}, u32[]{:S(2)}) copy-start(f32[192,768]{1,0:T(8,128)} %get-tuple-element.77) | copy-start | bytes 1769476
  518.8 6.7 %copy-start.15 = (f32[768,768]{1,0:T(8,128)S(1)}, f32[768,768]{1,0:T(8,128)}, u32[]{:S(2)}) copy-start(f32[768,768]{1,0:T(8,128)} %get-tuple-element.81) | copy-start | bytes 7077892
  (45 other events, 107.2 us)
Sparse Core Ops, SparseCore 0:
  13.8 22.3 all-gather.4
  54.0 28.0 reduce-scatter.4
  88.0 19.6 all-gather.6
  109.7 19.6 all-gather.8
  145.1 27.9 reduce-scatter.8
  176.1 28.0 reduce-scatter.6
  209.3 19.6 all-gather.10
  251.6 27.9 reduce-scatter.10
  285.8 232.9 all-reduce.4
where the time goes:
time: 544 us; the launch traced here: 535 us
  waiting for transfers between devices  326 us (60%)
  matrix products  64.6 us (12%)
  blocking collectives  63.9 us (12%)
  other arithmetic  42.8 us (8%)
  local copies, waits for them, and re-layouts  21.6 us (4%)
  between operations  14.8 us (3%)
    psum x1, waiting for transfers between devices, per_device(): lax.psum((query_weight_grad, query_bias_grad, key_weight_grad, value_weig...  184 us
    psum x1, blocking collectives, per_device(): lax.psum((gain_one_grad, shift_one_grad, out_bias_grad, gain_two_grad, sh...  41.8 us
    reduce_scatter x1, waiting for transfers between devices, per_device(): lax.psum_scatter(jnp.dot(activated, down_weight, preferred_element_type=f...  27.7 us
    reduce_scatter x1, waiting for transfers between devices, per_device(): lax.psum_scatter(jnp.dot(context, out_weight, preferred_element_type=f32)...  23.9 us
    psum x1, blocking collectives, per_device(): lax.psum((query_weight_grad, query_bias_grad, key_weight_grad, value_weig...  22.2 us
    reduce_scatter x1, waiting for transfers between devices, per_device(): lax.psum_scatter(jnp.einsum('rf,df->rd', hidden_grad, up_weight, preferre...  19.7 us
    unnamed x142, local copies, waits for them, and re-layouts  18.9 us
    all_gather x1, waiting for transfers between devices, per_device(): normed_all = lax.all_gather(normed, 'mp', axis=0, tiled=True)  18.7 us
  transfers between devices with their start and end apart: 9, of which 8 were waited for; matrix products, arithmetic and copies ran while one was open for 8% of the time, Pallas kernels for 0%

commit v1 on v0

--- a/solution.py
+++ b/solution.py
@@ -3,9 +3,19 @@
 import jax.numpy as jnp
 from jax import lax
 from jax.sharding import PartitionSpec as P
+from jax.lax import axis_index, axis_size, ppermute
 
 HD = 64
 eps = 1e-06
+
+
+def treat_strings_in(buf, array_axis):
+    buf = jnp.moveaxis(buf, 0, array_axis)
+    after = buf.shape
+    top = buf.reshape(
+        *after[:array_axis], after[array_axis] * after[array_axis + 1], *after[array_axis + 2 :]
+    )
+    return top
 
 
 def layer_norm(values, scaling, bias_add):
@@ -99,7 +109,18 @@
     ).astype(jnp.float32) + out_bias.astype(f32)
     middle = inputs + keep_rows[:, 0:1] * attended
     normed_two = layer_norm(middle, gain_two, shift_two).astype(bf16)
-    normed_two_all = lax.all_gather(normed_two, "mp", axis=0, tiled=True)
+    slots = axis_size("mp")
+    crops = []
+    for kk in [*range(slots)]:
+        crops.append((kk, (kk + 1) % slots))
+    nodes = [normed_two]
+    while len(nodes) < slots:
+        heard = ppermute(nodes[-1], axis_name="mp", perm=crops)
+        nodes.append(heard)
+    last = axis_index("mp")
+    kept_arr = jnp.stack(nodes)
+    nodes = kept_arr[(last - jnp.arange(slots)) % slots]
+    normed_two_all = treat_strings_in(nodes, 0)
     hidden = jnp.dot(normed_two_all, up_weight, preferred_element_type=f32) + up_bias.astype(f32)
     activated = gelu_exact(hidden).astype(bf16)
     mlp_out = lax.psum_scatter(

time: 544 us -> 538 us (0.989)
  waiting for transfers between devices: 326 us -> 318 us
    ppermute x0 -> x3, waiting for transfers between devices: none -> 26.9 us  [per_device(): heard = ppermute(nodes[-1], axis_name='mp', perm=crops)]
    all_gather x1 -> x0, waiting for transfers between devices: 16.9 us -> none  [per_device(): normed_two_all = lax.all_gather(normed_two, 'mp', axis=0, tiled=True)]
    all_gather x1, waiting for transfers between devices: 16.9 us -> 0.01 us  [per_device(): lax.all_gather(mlp_grad.astype(bf16), 'mp', axis=0, tiled=True)]
    unnamed x142 -> x144, local copies, waits for them, and re-layouts: 18.9 us -> 17.7 us
  transfers between devices with their start and end apart: 9 -> 11, of which waited for: 8 -> 9; matrix products, arithmetic and copies ran while one was open for 8% -> 10% of each run, Pallas kernels for 0% -> 0%
where the time goes in v1:
time: 538 us; the launch traced here: 529 us
  waiting for transfers between devices  318 us (59%)
  matrix products  64.6 us (12%)
  blocking collectives  64 us (12%)
  other arithmetic  42.1 us (8%)
  local copies, waits for them, and re-layouts  23.5 us (4%)
  between operations  15.2 us (3%)
    psum x1, waiting for transfers between devices, per_device(): lax.psum((query_weight_grad, query_bias_grad, key_weight_grad, value_weig...  184 us
    psum x1, blocking collectives, per_device(): lax.psum((gain_one_grad, shift_one_grad, out_bias_grad, gain_two_grad, sh...  41.8 us
    reduce_scatter x1, waiting for transfers between devices, per_device(): lax.psum_scatter(jnp.dot(activated, down_weight, preferred_element_type=f...  27.1 us
    ppermute x3, waiting for transfers between devices, per_device(): heard = ppermute(nodes[-1], axis_name='mp', perm=crops)  26.9 us
    reduce_scatter x1, waiting for transfers between devices, per_device(): lax.psum_scatter(jnp.dot(context, out_weight, preferred_element_type=f32)...  23.5 us
    psum x1, blocking collectives, per_device(): lax.psum((query_weight_grad, query_bias_grad, key_weight_grad, value_weig...  22.2 us
    reduce_scatter x1, waiting for transfers between devices, per_device(): lax.psum_scatter(jnp.einsum('rf,df->rd', hidden_grad, up_weight, preferre...  19.6 us
    all_gather x1, waiting for transfers between devices, per_device(): normed_all = lax.all_gather(normed, 'mp', axis=0, tiled=True)  18.7 us
  transfers between devices with their start and end apart: 11, of which 9 were waited for; matrix products, arithmetic and copies ran while one was open for 10% of the time, Pallas kernels for 0%

profile of v1, /device:TPU:0, one launch (start us, length us, event | category | flops | bytes accessed | tf_op | source)
XLA Modules:
  0.0 528.9 jit_solution(7641542765944824402)
XLA Ops:
  11.6 2.0 fusion.43
  17.5 18.7 %all-gather.4.cloned.1.call-done = bf16[1024,768]{1,0:T(8,128)(2,1)} async-done(((bf16[256,768]{1,0:T(8,128)(2,1)}), bf16[1024,768]{1,0:T(8,128)(2,1)}) %all-gather.4.cloned.1.call-update) | async-done | bytes 1572880 | tf_op jit(solution)/shard_map/all_gather | solution.py:74
  36.2 2.3 fusion.27
  58.5 23.5 %reduce-scatter.5.cloned.1.call-done = bf16[256,768]{1,0:T(8,128)(2,1)} async-done(((bf16[1024,768]{1,0:T(8,128)(2,1)}), bf16[256,768]{1,0:T(8,128)(2,1)}) %reduce-scatter.5.cloned.1.call-update) | async-done | bytes 393232 | tf_op jit(solution)/shard_map/reduce_scatter | solution.py:104
  86.0 7.2 %collective-permute-done = bf16[256,768]{1,0:T(8,128)(2,1)S(1)} collective-permute-done((bf16[256,768]{1,0:T(8,128)(2,1)S(1)}, bf16[256,768]{1,0:T(8,128)(2,1)S(1)}, u32[]{:S(2)}, u32[]{:S(2)}) %collective-permute-start) | collective-permute-done | bytes 393248 | tf_op jit(solution)/shard_map/ppermute | solution.py:118
  93.2 13.3 %collective-permute-done.1 = bf16[256,768]{1,0:T(8,128)(2,1)S(1)} collective-permute-done((bf16[256,768]{1,0:T(8,128)(2,1)S(1)}, bf16[256,768]{1,0:T(8,128)(2,1)S(1)}, u32[]{:S(2)}, u32[]{:S(2)}) %collective-permute-start.1) | collective-permute-done | bytes 393248 | tf_op jit(solution)/shard_map/ppermute | solution.py:118
  107.6 6.5 %collective-permute-done.2 = bf16[256,768]{1,0:T(8,128)(2,1)S(1)} collective-permute-done((bf16[256,768]{1,0:T(8,128)(2,1)S(1)}, bf16[256,768]{1,0:T(8,128)(2,1)S(1)}, u32[]{:S(2)}, u32[]{:S(2)}) %collective-permute-start.2) | collective-permute-done | bytes 393248 | tf_op jit(solution)/shard_map/ppermute | solution.py:118
  115.4 3.2 gather_fusion
  118.6 4.8 fusion.68
  123.4 11.9 %convert_reduce_fusion = (f32[768]{0:T(1024)}, bf16[1024,768]{1,0:T(8,128)(2,1)S(1)}, f32[1024,768]{1,0:T(8,128)}) fusion(f32[1024,768]{1,0:T(8,128)} %fusion.68, f32[768]{0:T(1024)S(1)} %convert_element_type.170, bf16[1024,768]{1,0:T(8,128)(2,1)} %all-gather.6.cloned.1.call-done, bf16[768,768]{1,0:T(8,128)(2,1)S(1)} %copy-done), kind=kOutput, calls=%fused_computation.21 | convolution fusion | flops 1266941184 | bytes 10622976 | tf_op jit(solution)/shard_map/rd,fd->rf/dot_general | solution.py:138
  136.4 2.6 convolution_convert_fusion
  139.1 3.3 multiply_convert_fusion.2
  143.5 2.6 convolution_convert_fusion.1
  147.6 19.6 %reduce-scatter.9.cloned.1.call-done = bf16[256,768]{1,0:T(8,128)(2,1)} async-done(((bf16[1024,768]{1,0:T(8,128)(2,1)}), bf16[256,768]{1,0:T(8,128)(2,1)}) %reduce-scatter.9.cloned.1.call-update) | async-done | bytes 393232 | tf_op jit(solution)/shard_map/reduce_scatter | solution.py:145
  167.2 2.1 fusion.47
  170.5 27.1 %reduce-scatter.7.cloned.1.call-done = bf16[256,768]{1,0:T(8,128)(2,1)} async-done(((bf16[1024,768]{1,0:T(8,128)(2,1)}), bf16[256,768]{1,0:T(8,128)(2,1)}) %reduce-scatter.7.cloned.1.call-update) | async-done | bytes 393232 | tf_op jit(solution)/shard_map/reduce_scatter | solution.py:126
  197.6 2.6 fusion.61
  200.2 2.3 fusion.36
  204.2 18.1 %all-gather.8.cloned.1.call-done = bf16[1024,768]{1,0:T(8,128)(2,1)} async-done(((bf16[256,768]{1,0:T(8,128)(2,1)}), bf16[1024,768]{1,0:T(8,128)(2,1)}) %all-gather.8.cloned.1.call-update) | async-done | bytes 1572880 | tf_op jit(solution)/shard_map/all_gather | solution.py:158
  222.4 2.1 convolution_convert_fusion.3
  224.5 3.9 multiply_reduce_fusion.1
  233.6 1.9 multiply_reduce_fusion
  235.6 1.8 convert_reduce_fusion.4
  245.1 4.9 fusion.72
  250.0 2.8 fusion.73
  258.9 22.2 %all-reduce.1 = (f32[192]{0:T(256)}, f32[192]{0:T(256)}, f32[768]{0:T(1024)}) all-reduce(f32[192]{0:T(256)S(1)} %reduce_sum.217, f32[192]{0:T(256)S(1)} %reduce_sum.219, f32[768]{0:T(1024)S(1)} %copy-done.60), channel_id=1, replica_groups=mesh['dp'=8,'mp'=4] {'dp'}, use_global_device_ids=true, to_apply=%region_24.25 | all-reduce | flops 1152 | bytes 9216 | tf_op jit(solution)/shard_map/psum | solution.py:232
  284.0 41.8 %all-reduce = (f32[768]{0:T(1024)}, f32[768]{0:T(1024)}, f32[768]{0:T(1024)}, f32[768]{0:T(1024)}, f32[768]{0:T(1024)}, /*index=5*/f32[768]{0:T(1024)}) all-reduce(f32[768]{0:T(1024)S(1)} %get-tuple-element.19, f32[768]{0:T(1024)S(1)} %get-tuple-element.24, f32[768]{0:T(1024)S(1)} %copy-done.51, ...), channel_id=1, replica_groups=mesh['dp'=8,'mp'=4] {'dp','mp'}, use_global_device_ids=true, to_apply=%region_19.20 | all-reduce | flops 4608 | bytes 36864 | tf_op jit(solution)/shard_map/psum | solution.py:247
  325.8 2.3 add_add_fusion.2
  328.1 184.2 %all-reduce.5.cloned.1.call-done = (f32[768,192]{0,1:T(8,128)}, f32[768,192]{0,1:T(8,128)}, f32[768,192]{0,1:T(8,128)}, f32[192,768]{1,0:T(8,128)}, f32[768,768]{1,0:T(8,128)}, /*index=5*/f32[768,768]{1,0:T(8,128)}) async-done(((f32[768,192]{0,1:T(8,128)}, f32[768,192]{0,1:T(8,128)}, f32[768,192]{0,1:T(8,128)}, f32[192,768]{1,0:T(8,128)}, f32[768,768]{1,0:T(8,128)}, /*index=5*/f32[768,768]{1,0:T(8,128)}), ...) | async-done | bytes 7077904 | tf_op jit(solution)/shard_map/psum | solution.py:232
  512.3 2.1 copy.42
  514.4 1.9 copy.43
  516.3 1.9 copy.44
  (227 shorter events, 66.4 us)
Async XLA Ops:
  7.2 116.2 %copy-start = (bf16[768,768]{1,0:T(8,128)(2,1)S(1)}, bf16[768,768]{1,0:T(8,128)(2,1)}, u32[]{:S(2)}) copy-start(bf16[768,768]{1,0:T(8,128)(2,1)} %param.35) | copy-start | bytes 3538948
  7.2 29.0 %all-gather.4.cloned.1.call-start = ((), (), s32[]{:S(2)}) async-start(), calls=%async_computation.4 | async-start | bytes 1966080 | tf_op jit(solution)/shard_map/all_gather | solution.py:74
  13.7 68.3 %reduce-scatter.5.cloned.1.call-start = ((), (), s32[]{:S(2)}) async-start(), calls=%async_computation.5 | async-start | bytes 1966080 | tf_op jit(solution)/shard_map/reduce_scatter | solution.py:104
  15.0 23.4 %copy-start.35 = (bf16[768,192]{0,1:T(8,128)(2,1)S(1)}, bf16[768,192]{0,1:T(8,128)(2,1)}, u32[]{:S(2)}) copy-start(bf16[768,192]{0,1:T(8,128)(2,1)} %param.26) | copy-start | bytes 884740
  51.3 30.6 %copy-start.4 = (bf16[256,768]{1,0:T(8,128)(2,1)S(1)}, bf16[256,768]{1,0:T(8,128)(2,1)}, u32[]{:S(2)}) copy-start(bf16[256,768]{1,0:T(8,128)(2,1)} %param.19) | copy-start | bytes 1179652
  53.8 69.6 %all-gather.6.cloned.1.call-start = ((), (), s32[]{:S(2)}) async-start(), calls=%async_computation.7 | async-start | bytes 1966080 | tf_op jit(solution)/shard_map/all_gather | solution.py:136
  57.0 110.2 %reduce-scatter.9.cloned.1.call-start = ((), (), s32[]{:S(2)}) async-start(), calls=%async_computation.8 | async-start | bytes 1966080 | tf_op jit(solution)/shard_map/reduce_scatter | solution.py:145
  83.2 30.9 %copy-start.45 = (f32[256]{0:T(256)}, f32[256]{0:T(256)S(1)}, u32[]{:S(2)}) copy-start(f32[256]{0:T(256)S(1)} %broadcast_multiply_fusion) | copy-start | bytes 3076
  84.6 34.1 %copy-start.58 = (f32[256]{0:T(256)}, f32[256]{0:T(256)S(1)}, u32[]{:S(2)}) copy-start(f32[256]{0:T(256)S(1)} %multiply_reduce_fusion.2) | copy-start | bytes 3076
  84.6 34.0 %copy-start.52 = (f32[256]{0:T(256)}, f32[256]{0:T(256)S(1)}, u32[]{:S(2)}) copy-start(f32[256]{0:T(256)S(1)} %fusion.54) | copy-start | bytes 3076
  85.9 7.3 %collective-permute-start = (bf16[256,768]{1,0:T(8,128)(2,1)S(1)}, bf16[256,768]{1,0:T(8,128)(2,1)S(1)}, u32[]{:S(2)}, u32[]{:S(2)}) collective-permute-start(bf16[256,768]{1,0:T(8,128)(2,1)S(1)} %add_convert_fusion.3), channel_id=1, source_target_pairs={{0,1},{1,2},{2,3},{3,0},{4,5},{5,6},{6,7},{7,4},{8,9},{9,10},{10,1... | collective-permute-start | bytes 1179656 | tf_op jit(solution)/shard_map/ppermute | solution.py:118
  93.2 13.3 %collective-permute-start.1 = (bf16[256,768]{1,0:T(8,128)(2,1)S(1)}, bf16[256,768]{1,0:T(8,128)(2,1)S(1)}, u32[]{:S(2)}, u32[]{:S(2)}) collective-permute-start(bf16[256,768]{1,0:T(8,128)(2,1)S(1)} %collective-permute-done), channel_id=1, source_target_pairs={{0,1},{1,2},{2,3},{3,0},{4,5},{5,6},{6,7},{7,4},{8,9},{9,10},{10,1... | collective-permute-start | bytes 1179656 | tf_op jit(solution)/shard_map/ppermute | solution.py:118
  106.4 7.6 %collective-permute-start.2 = (bf16[256,768]{1,0:T(8,128)(2,1)S(1)}, bf16[256,768]{1,0:T(8,128)(2,1)S(1)}, u32[]{:S(2)}, u32[]{:S(2)}) collective-permute-start(bf16[256,768]{1,0:T(8,128)(2,1)S(1)} %collective-permute-done.1), channel_id=1, source_target_pairs={{0,1},{1,2},{2,3},{3,0},{4,5},{5,6},{6,7},{7,4},{8,9},{9,10},{10,1... | collective-permute-start | bytes 1179656 | tf_op jit(solution)/shard_map/ppermute | solution.py:118
  123.4 13.0 %copy-start.63 = (bf16[768,768]{1,0:T(8,128)(2,1)S(1)}, bf16[768,768]{1,0:T(8,128)(2,1)}, u32[]{:S(2)}) copy-start(bf16[768,768]{1,0:T(8,128)(2,1)} %param.33) | copy-start | bytes 3538948
  139.0 58.6 %reduce-scatter.7.cloned.1.call-start = ((), (), s32[]{:S(2)}) async-start(), calls=%async_computation.6 | async-start | bytes 1966080 | tf_op jit(solution)/shard_map/reduce_scatter | solution.py:126
  143.5 23.7 %copy-start.6 = (bf16[256,768]{1,0:T(8,128)(2,1)S(1)}, bf16[256,768]{1,0:T(8,128)(2,1)}, u32[]{:S(2)}) copy-start(bf16[256,768]{1,0:T(8,128)(2,1)} %reduce-scatter.5.cloned.1.call-done) | copy-start | bytes 1179652
  146.1 54.1 %copy-start.12 = (bf16[256,768]{1,0:T(8,128)(2,1)S(1)}, bf16[256,768]{1,0:T(8,128)(2,1)}, u32[]{:S(2)}) copy-start(bf16[256,768]{1,0:T(8,128)(2,1)} %param.37) | copy-start | bytes 1179652
  146.1 76.2 %all-gather.8.cloned.1.call-start = ((), (), s32[]{:S(2)}) async-start(), calls=%async_computation.9 | async-start | bytes 1966080 | tf_op jit(solution)/shard_map/all_gather | solution.py:158
  200.2 24.3 %copy-start.23 = (bf16[1024,192]{0,1:T(8,128)(2,1)S(1)}, bf16[1024,192]{0,1:T(8,128)(2,1)}, u32[]{:S(2)}) copy-start(bf16[1024,192]{0,1:T(8,128)(2,1)} %copy-done.22) | copy-start | bytes 1179652
  202.6 78.5 %reduce-scatter.11.cloned.1.call-start = ((), (), s32[]{:S(2)}) async-start(), calls=%async_computation.10 | async-start | bytes 1966080 | tf_op jit(solution)/shard_map/reduce_scatter | solution.py:210
  244.8 267.4 %all-reduce.5.cloned.1.call-start = ((), (), s32[]{:S(2)}) async-start(), calls=%async_computation.11 | async-start | bytes 14155776 | tf_op jit(solution)/shard_map/psum | solution.py:232
  258.1 23.0 %copy-start.39 = (f32[768]{0:T(1024)S(1)}, f32[768]{0:T(1024)}, u32[]{:S(2)}) copy-start(f32[768]{0:T(1024)} %copy-done.38) | copy-start | bytes 9220
  258.1 23.0 %copy-start.42 = (f32[256]{0:T(256)S(1)}, f32[256]{0:T(256)}, u32[]{:S(2)}) copy-start(f32[256]{0:T(256)} %copy-done.41) | copy-start | bytes 3076
  258.1 24.3 %copy-start.57 = (f32[256]{0:T(256)S(1)}, f32[256]{0:T(256)}, u32[]{:S(2)}) copy-start(f32[256]{0:T(256)} %copy-done.56) | copy-start | bytes 3076
  258.1 24.3 %copy-start.47 = (f32[256]{0:T(256)S(1)}, f32[256]{0:T(256)}, u32[]{:S(2)}) copy-start(f32[256]{0:T(256)} %copy-done.46) | copy-start | bytes 3076
  258.1 25.8 %copy-start.48 = (f32[768]{0:T(1024)S(1)}, f32[768]{0:T(1024)}, u32[]{:S(2)}) copy-start(f32[768]{0:T(1024)} %get-tuple-element.17) | copy-start | bytes 9220
  258.1 25.8 %copy-start.49 = (f32[768]{0:T(1024)S(1)}, f32[768]{0:T(1024)}, u32[]{:S(2)}) copy-start(f32[768]{0:T(1024)} %get-tuple-element.23) | copy-start | bytes 9220
  258.1 25.8 %copy-start.50 = (f32[768]{0:T(1024)S(1)}, f32[768]{0:T(1024)}, u32[]{:S(2)}) copy-start(f32[768]{0:T(1024)} %get-tuple-element.21) | copy-start | bytes 9220
  258.1 25.8 %copy-start.51 = (f32[768]{0:T(1024)S(1)}, f32[768]{0:T(1024)}, u32[]{:S(2)}) copy-start(f32[768]{0:T(1024)} %get-tuple-element.22) | copy-start | bytes 9220
  258.2 67.6 %copy-start.13 = (bf16[256,768]{1,0:T(8,128)(2,1)S(1)}, bf16[256,768]{1,0:T(8,128)(2,1)}, u32[]{:S(2)}) copy-start(bf16[256,768]{1,0:T(8,128)(2,1)} %param.37) | copy-start | bytes 1179652
  258.2 67.6 %copy-start.55 = (f32[256]{0:T(256)S(1)}, f32[256]{0:T(256)}, u32[]{:S(2)}) copy-start(f32[256]{0:T(256)} %copy-done.54) | copy-start | bytes 3076
  512.3 6.7 %copy-start.15 = (f32[768,768]{1,0:T(8,128)S(1)}, f32[768,768]{1,0:T(8,128)}, u32[]{:S(2)}) copy-start(f32[768,768]{1,0:T(8,128)} %get-tuple-element.81) | copy-start | bytes 7077892
  (48 other events, 136.8 us)
Sparse Core Ops, SparseCore 0:
  13.8 22.3 all-gather.3
  53.9 27.9 reduce-scatter.4
  84.1 22.7 all-gather.5
  139.2 27.9 reduce-scatter.8
  169.6 27.9 reduce-scatter.6
  202.7 19.6 all-gather.7
  245.0 28.0 reduce-scatter.10
  279.3 232.9 all-reduce.4
